TPU v7x, 32 devices: a whole 2x2x4 slice. The times are simulated.
32 devices in a mesh: dp: 8 (over y, x, core), tensor: 4 (over z).
Axes of the slice: x: 2, y: 2, z: 4, core: 2. Of those that a mesh axis runs over, the one named last changes fastest.
Arguments:
- inputs: bfloat16 [18432, 768], P('dp'), may hold values from -6 to 6
- cotangent: bfloat16 [18432, 768], P('dp'), may hold values from -6 to 6, as said below
- row_expert: int32 [18432], P('dp'), may hold values from 0 to 2, as said below
- row_keep: int32 [18432], P('dp'), may hold values from 0 to 1, as said below
- window_resolution: int32 [24], P('dp'), may hold values from 0 to 1, as said below
- attention_norm_gain: float32 [768], replicated, may hold values from 0.5 to 1.5
- attention_norm_bias: float32 [768], replicated, may hold values from -0.6 to 0.6
- qkv_weight: bfloat16 [3, 768, 768], P(None, None, 'tensor'), may hold values from -0.21875 to 0.21875
- qv_bias: float32 [2, 12, 64], P(None, 'tensor'), may hold values from -1.8 to 1.8
- out_weight: bfloat16 [768, 768], P('tensor'), may hold values from -2.5 to 2.5
- out_bias: float32 [768], replicated, may hold values from -0.6 to 0.6
- second_gain: float32 [3, 768], replicated, may hold values from 0.5 to 1.5
- expert_norm_bias: float32 [3, 768], replicated, may hold values from -0.6 to 0.6
- up_weight: bfloat16 [3, 768, 3072], P(None, None, 'tensor'), may hold values from -0.21875 to 0.21875
- up_bias: float32 [3, 3072], P(None, 'tensor'), may hold values from -0.6 to 0.6
- down_weight: bfloat16 [3, 3072, 768], P(None, 'tensor'), may hold values from -0.109375 to 0.109375
- down_bias: float32 [3, 768], replicated, may hold values from -0.6 to 0.6
Outputs:
- layer_out: bfloat16 [18432, 768], P('dp')
- input_rows_gradient: bfloat16 [18432, 768], P('dp')
- attention_gain_gradient: float32 [768], replicated
- grad_first_bias: float32 [768], replicated
- grad_qkv: float32 [3, 768, 768], P(None, 'dp', 'tensor')
- grad_qv_bias: float32 [2, 12, 64], P(None, 'tensor')
- grad_out_weight: float32 [768, 768], P('tensor', 'dp')
- grad_out_bias: float32 [768], replicated
- expert_gain_gradient: float32 [3, 768], replicated
- grad_second_bias: float32 [3, 768], replicated
- grad_up: float32 [3, 768, 3072], P(None, 'dp', 'tensor')
- grad_up_bias: float32 [3, 3072], P(None, 'tensor')
- grad_down: float32 [3, 3072, 768], P(None, 'tensor', 'dp')
- grad_down_bias: float32 [3, 768], replicated
Inputs may be any that keep to these rules, and one draw needn't show every extreme that they name: `row_expert`: rows come in windows of 768 slots. A window with window_resolution = 1 holds one pair: 577 image rows, then 1 to 64 text rows, then padding. One with 0 holds two pairs, one in each half of 384 slots, each of 197 image rows, then 1 to 64 text rows, then padding. In some pairs every real row uses expert 2; otherwise image rows use 0 and text rows 1. Padding rows use 1. `row_keep`: 1 on the image and text rows of a pair, 0 on its padding; every pair has padding and its first row is real. `window_resolution`: all windows of one index of dp have the same value. `cotangent`: 0 on every row with row_keep = 0.
All inputs are finite; a program needn't handle non-finite values.
Results may differ from a plain program's by a relative error of at most 0.015.
Values may be sent and summed in bfloat16 or wider, within the bound.
No kernel may reach another device: no remote copies, remote signals or barrier semaphores. Data moves between devices by JAX's collectives and lax.ppermute only.
A program may use at most 256 MiB of HBM per device.

v0:
```python
import math
import jax
import jax.numpy as jnp
from jax import lax
from jax.sharding import PartitionSpec as P

HEAD_DIM = 64
S = 768
BLK = 128
epsilon = 1e-05
masked_score = -1000000000.0


def gelu_exact(values):
    return jax.nn.gelu(values, approximate=False)


def apply_layer_norm(values):
    mean_row = jnp.mean(values, -1, keepdims=True)
    centred = values - mean_row
    variance = jnp.mean(centred * centred, -1, keepdims=True)
    inverse_deviation = lax.rsqrt(variance + epsilon)
    return (centred * inverse_deviation, inverse_deviation)


def norm_backward_pass(rowwise_gradient, centred_normalized, inverse_deviation, rowwise_gain):
    scaled_output = rowwise_gradient * rowwise_gain
    return inverse_deviation * (
        scaled_output
        - jnp.mean(scaled_output, -1, keepdims=True)
        - centred_normalized * jnp.mean(scaled_output * centred_normalized, -1, keepdims=True)
    )


def lookup_table_rows(table, expert_selector_float):
    result = jnp.zeros((expert_selector_float.shape[0], table.shape[1]), jnp.float32)
    for expert_id in range(table.shape[0]):
        result = (
            result + expert_selector_float[:, expert_id : expert_id + 1] * table[expert_id][None, :]
        )
    return result


def grouped_totals(expert_selector_float, values):
    return jnp.einsum("re,rd->ed", expert_selector_float, values, precision=lax.Precision.HIGHEST)


def total_rows(values):
    return lax.psum(values, "tensor")


def group_slots(onehot_int, row_count):
    expert_count = onehot_int.shape[1]
    counts = jnp.sum(onehot_int, 0)
    padded = (counts + BLK - 1) // BLK * BLK
    group_ends = jnp.cumsum(padded)
    group_starts = group_ends - padded
    row_ranks = jnp.cumsum(onehot_int, 0) - onehot_int
    row_slots = jnp.sum(onehot_int * (group_starts[None, :] + row_ranks), 1)
    block_count = row_count // BLK + expert_count - 1
    sources = jnp.full((block_count * BLK,), row_count, jnp.int32)
    sources = sources.at[row_slots].set(jnp.arange(row_count, dtype=jnp.int32))
    firsts = jnp.arange(block_count, dtype=jnp.int32) * BLK
    block_expert = jnp.minimum(
        jnp.sum((firsts[:, None] >= group_ends[None, :]).astype(jnp.int32), 1), expert_count - 1
    )
    return (row_slots, sources, block_expert)


def head_split(rows_in):
    return rows_in.reshape(rows_in.shape[0], rows_in.shape[1] // HEAD_DIM, HEAD_DIM)


def masked_scores(q_heads, k_heads, keep_rows, single):
    scale_factor = 1.0 / math.sqrt(HEAD_DIM)
    scores = (
        jnp.einsum("qhd,khd->hqk", q_heads, k_heads, preferred_element_type=jnp.float32)
        * scale_factor
    )
    positions = jnp.arange(keep_rows.shape[0], dtype=jnp.int32)
    upper = positions >= keep_rows.shape[0] // 2
    same_half = upper[:, None] == upper[None, :]
    allowed = (keep_rows[None, :] > 0) & (same_half | (single > 0))
    return jnp.where(allowed[None, :, :], scores, masked_score)


def attend_forward(pieces):
    query_rows, key_rows, value_rows, keep_rows, single = pieces
    q_heads, k_heads, v_heads = (
        head_split(query_rows),
        head_split(key_rows),
        head_split(value_rows),
    )
    scores = masked_scores(q_heads, k_heads, keep_rows, single)
    row_max = jnp.max(scores, -1, keepdims=True)
    exp_scores = jnp.exp(scores - row_max)
    exp_total = jnp.sum(exp_scores, -1, keepdims=True)
    weights = (exp_scores / exp_total).astype(jnp.bfloat16)
    log_totals = row_max[..., 0] + jnp.log(exp_total[..., 0])
    mixed_heads = jnp.einsum("hqk,khd->qhd", weights, v_heads, preferred_element_type=jnp.float32)
    return (mixed_heads.astype(jnp.bfloat16).reshape(query_rows.shape), log_totals)


def attend_backward(pieces):
    query_rows, key_rows, value_rows, keep_rows, single, log_totals, rowwise_gradient = pieces
    scale_factor = 1.0 / math.sqrt(HEAD_DIM)
    q_heads, k_heads, v_heads = (
        head_split(query_rows),
        head_split(key_rows),
        head_split(value_rows),
    )
    grad_heads = head_split(rowwise_gradient)
    scores = masked_scores(q_heads, k_heads, keep_rows, single)
    probs = jnp.exp(scores - log_totals[..., None])
    weights = probs.astype(jnp.bfloat16)
    grad_value = jnp.einsum("hqk,qhd->khd", weights, grad_heads, preferred_element_type=jnp.float32)
    grad_probs = jnp.einsum("qhd,khd->hqk", grad_heads, v_heads, preferred_element_type=jnp.float32)
    grad_scores = probs * (grad_probs - jnp.sum(probs * grad_probs, -1, keepdims=True))
    grad_scores = grad_scores.astype(jnp.bfloat16)
    grad_query = (
        jnp.einsum("hqk,khd->qhd", grad_scores, k_heads, preferred_element_type=jnp.float32)
        * scale_factor
    )
    grad_key = (
        jnp.einsum("hqk,qhd->khd", grad_scores, q_heads, preferred_element_type=jnp.float32)
        * scale_factor
    )
    return (
        grad_query.astype(jnp.bfloat16).reshape(query_rows.shape),
        grad_key.astype(jnp.bfloat16).reshape(query_rows.shape),
        grad_value.astype(jnp.bfloat16).reshape(query_rows.shape),
    )


def body(
    inputs,
    cotangent,
    row_expert,
    row_keep,
    window_resolution,
    attention_norm_gain,
    attention_norm_bias,
    qkv_weight,
    qv_bias,
    out_weight,
    out_bias,
    second_gain,
    expert_norm_bias,
    up_weight,
    up_bias,
    down_weight,
    down_bias,
):
    row_count, model_width = inputs.shape
    expert_count = up_weight.shape[0]
    local_width = qkv_weight.shape[2]
    seq_count = row_count // S
    share_count = row_count // lax.axis_size("tensor")
    share_start = lax.axis_index("tensor") * share_count

    def local_row_block(values):
        return lax.dynamic_slice_in_dim(values, share_start, share_count, 0)

    gathered_source_rows = inputs.astype(jnp.float32)
    onehot_int = (row_expert[:, None] == jnp.arange(expert_count, dtype=jnp.int32)[None, :]).astype(
        jnp.int32
    )
    expert_selector_float = onehot_int.astype(jnp.float32)
    expert_selector_local = local_row_block(expert_selector_float)
    attention_centred, attention_inverse_deviation = apply_layer_norm(gathered_source_rows)
    attention_normed = (attention_centred * attention_norm_gain + attention_norm_bias).astype(
        jnp.bfloat16
    )
    bias_pair = qv_bias.reshape(2, local_width)
    query = (
        jnp.dot(attention_normed, qkv_weight[0], preferred_element_type=jnp.float32) + bias_pair[0]
    ).astype(jnp.bfloat16)
    keyed = jnp.dot(attention_normed, qkv_weight[1], preferred_element_type=jnp.float32).astype(
        jnp.bfloat16
    )
    valued = (
        jnp.dot(attention_normed, qkv_weight[2], preferred_element_type=jnp.float32) + bias_pair[1]
    ).astype(jnp.bfloat16)
    seq_query = query.reshape(seq_count, S, local_width)
    seq_key = keyed.reshape(seq_count, S, local_width)
    seq_value = valued.reshape(seq_count, S, local_width)
    seq_keep = row_keep.reshape(seq_count, S)
    mixed_seq, log_totals = lax.map(
        attend_forward, (seq_query, seq_key, seq_value, seq_keep, window_resolution)
    )
    mixed = mixed_seq.reshape(row_count, local_width)
    attn_part = jnp.dot(mixed, out_weight, preferred_element_type=jnp.float32)
    residual_hidden = gathered_source_rows + (total_rows(attn_part) + out_bias)
    expert_centred, expert_inverse_deviation = apply_layer_norm(residual_hidden)
    rowwise_gain = lookup_table_rows(second_gain, expert_selector_float)
    expert_normed = (
        expert_centred * rowwise_gain + lookup_table_rows(expert_norm_bias, expert_selector_float)
    ).astype(jnp.bfloat16)
    expert_centred_local = local_row_block(expert_centred)
    row_slots, sources, block_expert = group_slots(onehot_int, row_count)
    block_count = block_expert.shape[0]
    zero_row = jnp.zeros((1, model_width), jnp.bfloat16)
    hidden_in = jnp.concatenate([expert_normed, zero_row], 0)[sources].reshape(
        block_count, BLK, model_width
    )

    def expert_block(pieces):
        block_in, expert_id = pieces
        up_mat = lax.dynamic_index_in_dim(up_weight, expert_id, 0, keepdims=False)
        down_mat = lax.dynamic_index_in_dim(down_weight, expert_id, 0, keepdims=False)
        up_row = lax.dynamic_index_in_dim(up_bias, expert_id, 0, keepdims=False)
        pre_act = jnp.dot(block_in, up_mat, preferred_element_type=jnp.float32) + up_row
        act_out = gelu_exact(pre_act).astype(jnp.bfloat16)
        block_out = jnp.dot(act_out, down_mat, preferred_element_type=jnp.float32)
        return (pre_act, act_out, block_out)

    pre_blocks, act_blocks, out_blocks = lax.map(expert_block, (hidden_in, block_expert))
    expert_part = out_blocks.reshape(block_count * BLK, model_width)[row_slots]
    layer_out = (
        residual_hidden
        + (total_rows(expert_part) + lookup_table_rows(down_bias, expert_selector_float))
    ).astype(jnp.bfloat16)
    cot_own = local_row_block(cotangent).astype(jnp.float32)
    grad_down_bias = grouped_totals(expert_selector_local, cot_own)
    grad_in_blocks = jnp.concatenate([cotangent, zero_row], 0)[sources].reshape(
        block_count, BLK, model_width
    )

    def expert_back(running, pieces):
        acc_up, acc_down, acc_up_bias = running
        block_in, pre_act, act_out, grad_block, expert_id = pieces
        up_mat = lax.dynamic_index_in_dim(up_weight, expert_id, 0, keepdims=False)
        down_mat = lax.dynamic_index_in_dim(down_weight, expert_id, 0, keepdims=False)
        grad_act = jnp.einsum("rd,fd->rf", grad_block, down_mat, preferred_element_type=jnp.float32)
        _, pullback = jax.vjp(gelu_exact, pre_act)
        grad_pre = pullback(grad_act)[0].astype(jnp.bfloat16)
        acc_up = acc_up.at[expert_id].add(
            jnp.einsum("rd,rf->df", block_in, grad_pre, preferred_element_type=jnp.float32)
        )
        acc_down = acc_down.at[expert_id].add(
            jnp.einsum("rf,rd->fd", act_out, grad_block, preferred_element_type=jnp.float32)
        )
        acc_up_bias = acc_up_bias.at[expert_id].add(jnp.sum(grad_pre.astype(jnp.float32), 0))
        grad_hidden = jnp.einsum("rf,df->rd", grad_pre, up_mat, preferred_element_type=jnp.float32)
        return ((acc_up, acc_down, acc_up_bias), grad_hidden)

    start_state = (
        jnp.zeros(up_weight.shape, jnp.float32),
        jnp.zeros(down_weight.shape, jnp.float32),
        jnp.zeros(up_bias.shape, jnp.float32),
    )
    (grad_up, grad_down, grad_up_bias), grad_hidden_blocks = lax.scan(
        expert_back, start_state, (hidden_in, pre_blocks, act_blocks, grad_in_blocks, block_expert)
    )
    hidden_part = grad_hidden_blocks.reshape(block_count * BLK, model_width)[row_slots]
    expert_normed_gradient = total_rows(hidden_part)
    residual_gradient = cotangent.astype(jnp.float32) + norm_backward_pass(
        expert_normed_gradient, expert_centred, expert_inverse_deviation, rowwise_gain
    )
    grad_attn = residual_gradient.astype(jnp.bfloat16)
    expert_normed_gradient_local = local_row_block(expert_normed_gradient)
    grad_attn_own = local_row_block(grad_attn)
    expert_gain_gradient = grouped_totals(
        expert_selector_local, expert_normed_gradient_local * expert_centred_local
    )
    grad_second_bias = grouped_totals(expert_selector_local, expert_normed_gradient_local)
    grad_out_bias = jnp.sum(grad_attn_own.astype(jnp.float32), 0)
    grad_out_weight = jnp.einsum("rh,rd->hd", mixed, grad_attn, preferred_element_type=jnp.float32)
    grad_mixed = jnp.einsum(
        "rd,hd->rh", grad_attn, out_weight, preferred_element_type=jnp.float32
    ).astype(jnp.bfloat16)
    grad_q_seq, grad_k_seq, grad_v_seq = lax.map(
        attend_backward,
        (
            seq_query,
            seq_key,
            seq_value,
            seq_keep,
            window_resolution,
            log_totals,
            grad_mixed.reshape(seq_count, S, local_width),
        ),
    )
    grad_query = grad_q_seq.reshape(row_count, local_width)
    grad_key = grad_k_seq.reshape(row_count, local_width)
    grad_value = grad_v_seq.reshape(row_count, local_width)
    grad_qkv = jnp.stack(
        [
            jnp.einsum("rd,rh->dh", attention_normed, grad_part, preferred_element_type=jnp.float32)
            for grad_part in (grad_query, grad_key, grad_value)
        ]
    )
    grad_qv_bias = jnp.stack(
        [jnp.sum(grad_query.astype(jnp.float32), 0), jnp.sum(grad_value.astype(jnp.float32), 0)]
    ).reshape(qv_bias.shape)
    first_part = jnp.einsum(
        "rh,dh->rd", grad_query, qkv_weight[0], preferred_element_type=jnp.float32
    )
    first_part = first_part + jnp.einsum(
        "rh,dh->rd", grad_key, qkv_weight[1], preferred_element_type=jnp.float32
    )
    first_part = first_part + jnp.einsum(
        "rh,dh->rd", grad_value, qkv_weight[2], preferred_element_type=jnp.float32
    )
    attention_centred_local = local_row_block(attention_centred)
    attention_normed_gradient = total_rows(first_part)
    input_rows_gradient = (
        residual_gradient
        + norm_backward_pass(
            attention_normed_gradient,
            attention_centred,
            attention_inverse_deviation,
            attention_norm_gain,
        )
    ).astype(jnp.bfloat16)
    attention_normed_gradient_local = local_row_block(attention_normed_gradient)
    attention_gain_gradient = jnp.sum(attention_normed_gradient_local * attention_centred_local, 0)
    grad_first_bias = jnp.sum(attention_normed_gradient_local, 0)
    summed_qkv, summed_out, summed_up, summed_down = (
        lax.psum_scatter(
            grad_qkv.astype(jnp.bfloat16), "dp", scatter_dimension=1, tiled=True
        ).astype(jnp.float32),
        lax.psum_scatter(
            grad_out_weight.astype(jnp.bfloat16), "dp", scatter_dimension=1, tiled=True
        ).astype(jnp.float32),
        lax.psum_scatter(
            grad_up.astype(jnp.bfloat16), "dp", scatter_dimension=1, tiled=True
        ).astype(jnp.float32),
        lax.psum_scatter(
            grad_down.astype(jnp.bfloat16), "dp", scatter_dimension=2, tiled=True
        ).astype(jnp.float32),
    )
    norm_sums = lax.psum(
        (
            attention_gain_gradient,
            grad_first_bias,
            grad_out_bias,
            expert_gain_gradient,
            grad_second_bias,
            grad_down_bias,
        ),
        ("dp", "tensor"),
    )
    small_sums = lax.psum((grad_qv_bias, grad_up_bias), "dp")
    return (
        layer_out,
        input_rows_gradient,
        norm_sums[0],
        norm_sums[1],
        summed_qkv,
        small_sums[0],
        summed_out,
        norm_sums[2],
        norm_sums[3],
        norm_sums[4],
        summed_up,
        small_sums[1],
        summed_down,
        norm_sums[5],
    )


def solution(mesh):
    in_specs = (
        P("dp", None),
        P("dp", None),
        P("dp"),
        P("dp"),
        P("dp"),
        P(),
        P(),
        P(None, None, "tensor"),
        P(None, "tensor", None),
        P("tensor", None),
        P(),
        P(),
        P(),
        P(None, None, "tensor"),
        P(None, "tensor"),
        P(None, "tensor", None),
        P(),
    )
    out_specs = (
        P("dp", None),
        P("dp", None),
        P(),
        P(),
        P(None, "dp", "tensor"),
        P(None, "tensor", None),
        P("tensor", "dp"),
        P(),
        P(),
        P(),
        P(None, "dp", "tensor"),
        P(None, "tensor"),
        P(None, "tensor", "dp"),
        P(),
    )
    return jax.shard_map(body, mesh=mesh, in_specs=in_specs, out_specs=out_specs, check_vma=False)
```

profile of v0, /device:TPU:0, one launch (start us, length us, event | category | flops | bytes accessed | tf_op | source)
XLA Modules:
  0.0 2110.5 jit_solution(14729037549028274431)
XLA Ops:
  13.2 5.3 fusion.82
  26.8 26.4 %while.59 = (s32[]{:T(128)}, bf16[3,768,192]{1,2,0:T(8,128)(2,1)}, f32[3,3,768]{2,1,0:T(4,128)}, bf16[3,768,192]{1,2,0:T(8,128)(2,1)S(1)}, s32[3,768]{1,0:T(4,12...) while((s32[]{:T(128)}, bf16[3,768,192]{1,2,0:T(8,128)(2,1)}, ...), condition=%wide.region_5.6_spmd, body=%wide.region_2.5_spmd.sunk | while | flops 476134656 | bytes 27215000 | solution.py:188
  66.1 9.0 scatter_custom_fusion
  75.1 13.0 gather_fusion.2
  89.1 222.3 %all-reduce.9.cloned.1.call-done = f32[2304,768]{1,0:T(8,128)} async-done(((f32[2304,768]{1,0:T(8,128)}), f32[2304,768]{1,0:T(8,128)}) %all-reduce.9.cloned.1.call-update) | async-done | bytes 7077904 | tf_op jit(solution)/shard_map/psum | solution.py:49
  311.3 5.2 fusion.127
  320.7 15.5 add_convert_fusion.2
  338.2 12.8 gather_fusion
  358.9 207.5 %while.60 = (s32[]{:T(128)}, f32[20,128,768]{2,1,0:T(8,128)}, bf16[20,128,768]{2,1,0:T(8,128)(2,1)}, f32[20,128,768]{2,1,0:T(8,128)}, bf16[20,128,768]{2,1,0:T(8...) while((s32[]{:T(128)}, f32[20,128,768]{2,1,0:T(8,128)}, ...), condition=%wide.region_17.18_spmd, body=%wide.region_16.17_spmd.sunk | while | flops 314867712 | bytes 4729531 | solution.py:217
  577.2 544.5 %while.61 = (s32[]{:T(128)}, f32[3,768,768]{2,1,0:T(8,128)}, f32[3,768,768]{1,2,0:T(8,128)}, f32[3,768]{1,0:T(4,128)S(1)}, f32[20,128,768]{2,1,0:T(8,128)}, /*in...) while((s32[]{:T(128)}, f32[3,768,768]{2,1,0:T(8,128)}, ...), condition=%wide.region_23.24_spmd, body=%wide.region_19.23_spmd.sunk | while | flops 613614336 | bytes 32857364 | solution.py:252
  1121.7 12.7 gather_fusion.3
  1134.4 5.6 convert_element_type.143
  1140.2 12.8 gather_fusion.1
  1153.0 5.4 convert_element_type.145
  1158.5 223.4 %all-reduce.11.cloned.1.call-done = f32[2304,768]{1,0:T(8,128)} async-done(((f32[2304,768]{1,0:T(8,128)}), f32[2304,768]{1,0:T(8,128)}) %all-reduce.11.cloned.1.call-update) | async-done | bytes 7077904 | tf_op jit(solution)/shard_map/psum | solution.py:49
  1381.8 8.2 fusion.128
  1390.5 8.0 fusion.129
  1401.3 51.2 %while.62 = (s32[]{:T(128)}, bf16[3,768,192]{1,2,0:T(8,128)(2,1)S(1)}, bf16[3,768,192]{1,2,0:T(8,128)(2,1)}, bf16[3,768,192]{1,2,0:T(8,128)(2,1)S(1)}, bf16[3,76...) while((s32[]{:T(128)}, ...), condition=%wide.region_29.30_spmd, body=%wide.region_27.29_spmd.sunk | while | flops 1161510144 | bytes 62592184 | solution.py:272
  1494.7 23.7 %all-reduce.3 = (f32[2,3,64]{2,1,0:T(4,128)S(1)}, f32[3,768]{1,0:T(4,128)}) all-reduce(f32[2,3,64]{2,1,0:T(4,128)S(1)} %pad_maximum_fusion.1, f32[3,768]{1,0:T(4,128)S(1)} %copy-done.23), channel_id=1, replica_groups=mesh['dp'=8,'tensor'=4] {'dp'}, use_global_device_ids=true, to_apply=%region_40.41 | all-reduce | flops 2688 | bytes 21504 | tf_op jit(solution)/shard_map/psum | solution.py:344
  1527.3 32.2 %reduce-scatter.13.cloned.1.call-done = bf16[96,576]{1,0:T(8,128)(2,1)} async-done(((bf16[768,576]{1,0:T(8,128)(2,1)}), bf16[96,576]{1,0:T(8,128)(2,1)}) %reduce-scatter.13.cloned.1.call-update) | async-done | bytes 110608
  1561.6 478.2 %all-reduce.13.cloned.1.call-done = (f32[2304,768]{1,0:T(8,128)}, f32[2304,768]{1,0:T(8,128)}) async-done(((f32[2304,768]{1,0:T(8,128)}, f32[2304,768]{1,0:T(8,128)}), (f32[2304,768]{1,0:T(8,128)}, f32[2304,768]{1,0:T(8,128)})) %all-reduce.13.cloned.1.call-update) | async-done | bytes 14155792 | tf_op jit(solution)/shard_map/psum | solution.py:49
  2039.8 5.5 multiply_reduce_fusion.4
  2047.6 40.5 %all-reduce.2 = (f32[768]{0:T(1024)}, f32[768]{0:T(1024)}, f32[768]{0:T(1024)}, f32[3,768]{1,0:T(4,128)}, f32[3,768]{1,0:T(4,128)}, /*index=5*/f32[3,768]{1,0:T(4,128)}) all-reduce(f32[768]{0:T(1024)S(1)} %get-tuple-element.415, f32[768]{0:T(1024)S(1)} %get-tuple-element.414, ...), channel_id=1, replica_groups=mesh['dp'=8,'tensor'=4] {'dp','tensor'}, use_global_device_ids=true, to_apply=%region_34.35 | all-reduce | flops 9216 | bytes 73728 | tf_op jit(solution)/shard_map/psum | solution.py:333
  2088.1 15.1 add_convert_fusion
  (634 shorter events, 846.6 us)
Async XLA Ops:
  7.2 48.9 %copy-start = (bf16[192,768]{1,0:T(8,128)(2,1)S(1)}, bf16[192,768]{1,0:T(8,128)(2,1)}, u32[]{:S(2)}) copy-start(bf16[192,768]{1,0:T(8,128)(2,1)} %param.40) | copy-start | bytes 884740
  7.2 304.1 %all-reduce.9.cloned.1.call-start = ((), (), s32[]{:S(2)}) async-start(), calls=%async_computation.4 | async-start | bytes 14155776 | tf_op jit(solution)/shard_map/psum | solution.py:49
  9.9 8.6 copy-start.14
  60.1 1321.7 %all-reduce.11.cloned.1.call-start = ((), (), s32[]{:S(2)}) async-start(), calls=%async_computation.5 | async-start | bytes 14155776 | tf_op jit(solution)/shard_map/psum | solution.py:49
  75.1 13.2 copy-start.31
  75.1 13.2 copy-start.32
  75.1 236.2 %copy-start.24 = (f32[768]{0:T(1024)S(1)}, f32[768]{0:T(1024)}, u32[]{:S(2)}) copy-start(f32[768]{0:T(1024)} %param.41) | copy-start | bytes 9220
  311.3 7.1 copy-start.2
  569.8 7.4 copy-start.28
  569.8 7.4 copy-start.29
  1121.7 12.7 copy-start.22
  1134.4 355.7 %reduce-scatter.9.cloned.1.call-start = ((), (), s32[]{:S(2)}) async-start(), calls=%async_computation.6 | async-start | bytes 3981312 | tf_op jit(solution)/shard_map/reduce_scatter | solution.py:326
  1140.1 352.0 %reduce-scatter.11.cloned.1.call-start = ((), (), s32[]{:S(2)}) async-start(), calls=%async_computation.7 | async-start | bytes 3981312 | tf_op jit(solution)/shard_map/reduce_scatter | solution.py:329
  1153.0 237.1 %slice-start = ((s8[7077888]{0:T(1024)(128)(4,1)}), s8[2883584]{0:T(1024)(128)(4,1)S(1)}, s32[]{:S(2)}) async-start(s8[7077888]{0:T(1024)(128)(4,1)} %bitcast.359), calls=%async_computation.11 | async-start | bytes 5767168
  1158.4 367.3 %reduce-scatter.15.cloned.1.call-start = ((), (), s32[]{:S(2)}) async-start(), calls=%async_computation.9 | async-start | bytes 442368
  1381.8 8.3 slice-start.1
  1381.8 8.7 copy-start.3
  1466.9 92.5 %reduce-scatter.13.cloned.1.call-start = ((), (), s32[]{:S(2)}) async-start(), calls=%async_computation.8 | async-start | bytes 1105920
  1479.8 560.0 %all-reduce.13.cloned.1.call-start = ((), (), s32[]{:S(2)}) async-start(), calls=%async_computation.10 | async-start | bytes 28311552 | tf_op jit(solution)/shard_map/psum | solution.py:49
  1487.6 7.1 copy-start.23
  1487.6 552.2 %copy-start.15 = (f32[2304]{0:T(1024)S(1)}, f32[2304]{0:T(1024)}, u32[]{:S(2)}) copy-start(f32[2304]{0:T(1024)} %copy-done.14) | copy-start | bytes 27652
  1487.6 552.2 %copy-start.19 = (f32[2304]{0:T(1024)S(1)}, f32[2304]{0:T(1024)}, u32[]{:S(2)}) copy-start(f32[2304]{0:T(1024)} %copy-done.18) | copy-start | bytes 27652
  1487.7 552.1 %copy-start.27 = (f32[768]{0:T(1024)S(1)}, f32[768]{0:T(1024)}, u32[]{:S(2)}) copy-start(f32[768]{0:T(1024)} %param.36) | copy-start | bytes 9220
  2039.8 48.3 %copy-start.25 = (f32[768]{0:T(1024)S(1)}, f32[768]{0:T(1024)}, u32[]{:S(2)}) copy-start(f32[768]{0:T(1024)} %param.41) | copy-start | bytes 9220
  (23 other events, 89.2 us)
Sparse Core Ops, SparseCore 0:
  60.2 251.0 all-reduce.8
  1134.5 247.2 all-reduce.10
  1385.3 46.9 reduce-scatter.8
  1435.7 48.0 reduce-scatter.10
  1486.7 33.8 reduce-scatter.14
  1523.6 35.7 reduce-scatter.12
  1562.2 477.5 all-reduce.12
where the time goes:
time: 2130 us; the launch traced here: 2110 us
  waiting for transfers between devices  956 us (45%)
  matrix products  450 us (21%)
  local copies, waits for them, and re-layouts  346 us (16%)
  other arithmetic  184 us (9%)
  loops' own time  94.3 us (4%)
  blocking collectives  64.2 us (3%)
    psum x3, waiting for transfers between devices, total_rows(): return lax.psum(values, 'tensor')  924 us
    another operation x50, local copies, waits for them, and re-layouts  126 us
    dot_general x20, matrix products, expert_back(): jnp.einsum('rd,rf->df', block_in, grad_pre, preferred_element_type=jnp.fl...  86.5 us
    scatter-add x40, local copies, waits for them, and re-layouts, expert_back(): acc_down.at[expert_id]  72.3 us
    dot_general x20, matrix products, expert_back(): jnp.einsum('rf,rd->fd', act_out, grad_block, preferred_element_type=jnp.f...  71.4 us
    dot_general x20, matrix products, expert_block(): block_out = jnp.dot(act_out, down_mat, preferred_element_type=jnp.float32)  62.2 us
    dot_general x20, matrix products, expert_back(): jnp.einsum('rd,fd->rf', grad_block, down_mat, preferred_element_type=jnp....  52.5 us
    dot_general x20, matrix products, expert_back(): jnp.einsum('rf,df->rd', grad_pre, up_mat, preferred_element_type=jnp.floa...  51.5 us
  transfers between devices with their start and end apart: 7, of which 4 were waited for; matrix products, arithmetic and copies ran while one was open for 8% of the time, Pallas kernels for 0%

commit v1 on v0

--- a/solution.py
+++ b/solution.py
@@ -1,3 +1,4 @@
+import functools
 import math
 import jax
 import jax.numpy as jnp
@@ -9,6 +10,14 @@
 BLK = 128
 epsilon = 1e-05
 masked_score = -1000000000.0
+
+
+def _take_plane(xin, axis_name):
+    aux = lax.all_gather(xin, axis_name=axis_name).sum(axis=0)
+    return aux
+
+
+order_edges = functools.partial(_take_plane, axis_name="tensor")
 
 
 def gelu_exact(values):
@@ -46,7 +55,7 @@
 
 
 def total_rows(values):
-    return lax.psum(values, "tensor")
+    return order_edges(values)
 
 
 def group_slots(onehot_int, row_count):

time: 2130 us -> 3080 us (1.45)
  waiting for transfers between devices: 956 us -> 1850 us
  other arithmetic: 184 us -> 243 us
    all_gather x0 -> x4, waiting for transfers between devices: none -> 1800 us  [_take_plane(): aux = lax.all_gather(xin, axis_name=axis_name).sum(axis=0)]
    psum x3 -> x0, waiting for transfers between devices: 924 us -> none  [total_rows(): return lax.psum(values, 'tensor')]
    reduce_sum x0 -> x4, other arithmetic: none -> 55.6 us  [_take_plane(): aux = lax.all_gather(xin, axis_name=axis_name).sum(axis=0)]
  transfers between devices with their start and end apart: 7 -> 8, of which waited for: 4 -> 6; matrix products, arithmetic and copies ran while one was open for 8% -> 7% of each run, Pallas kernels for 0% -> 0%
where the time goes in v1:
time: 3080 us; the launch traced here: 3060 us
  waiting for transfers between devices  1850 us (60%)
  matrix products  453 us (15%)
  local copies, waits for them, and re-layouts  351 us (11%)
  other arithmetic  243 us (8%)
  loops' own time  83.8 us (3%)
  blocking collectives  65.9 us (2%)
    all_gather x4, waiting for transfers between devices, _take_plane(): aux = lax.all_gather(xin, axis_name=axis_name).sum(axis=0)  1800 us
    another operation x50, local copies, waits for them, and re-layouts  126 us
    dot_general x20, matrix products, expert_back(): jnp.einsum('rd,rf->df', block_in, grad_pre, preferred_element_type=jnp.fl...  88 us
    scatter-add x40, local copies, waits for them, and re-layouts, expert_back(): acc_down.at[expert_id]  72.9 us
    dot_general x20, matrix products, expert_back(): jnp.einsum('rf,rd->fd', act_out, grad_block, preferred_element_type=jnp.f...  72.2 us
    dot_general x20, matrix products, expert_block(): block_out = jnp.dot(act_out, down_mat, preferred_element_type=jnp.float32)  62.2 us
  transfers between devices with their start and end apart: 8, of which 6 were waited for; matrix products, arithmetic and copies ran while one was open for 7% of the time, Pallas kernels for 0%

profile of v1, /device:TPU:0, one launch (start us, length us, event | category | flops | bytes accessed | tf_op | source)
XLA Modules:
  0.0 3060.7 jit_solution(8714686938573068212)
XLA Ops:
  28.9 26.4 while.59
  68.3 9.0 scatter_custom_fusion
  77.3 13.6 gather_fusion.2
  91.9 449.2 %all-gather.9.cloned.1.call-done = f32[9216,768]{1,0:T(8,128)} async-done(((f32[2304,768]{1,0:T(8,128)}), f32[9216,768]{1,0:T(8,128)}) %all-gather.9.cloned.1.call-update) | async-done | bytes 28311568 | tf_op jit(solution)/shard_map/all_gather | solution.py:16
  541.1 13.6 reduce_sum.211
  564.2 15.5 add_convert_fusion.2
  581.8 12.8 gather_fusion
  602.5 207.9 %while.60 = (s32[]{:T(128)}, f32[20,128,768]{2,1,0:T(8,128)}, bf16[20,128,768]{2,1,0:T(8,128)(2,1)}, f32[20,128,768]{2,1,0:T(8,128)}, bf16[20,128,768]{2,1,0:T(8...) while((s32[]{:T(128)}, f32[20,128,768]{2,1,0:T(8,128)}, ...), condition=%wide.region_17.18_spmd, body=%wide.region_16.17_spmd.sunk | while | flops 314867712 | bytes 4730031 | solution.py:226
  821.3 537.9 %while.61 = (s32[]{:T(128)}, f32[3,768,768]{2,1,0:T(8,128)}, f32[3,768,768]{1,2,0:T(8,128)}, f32[3,768]{1,0:T(4,128)S(1)}, f32[20,128,768]{2,1,0:T(8,128)}, /*in...) while((s32[]{:T(128)}, f32[3,768,768]{2,1,0:T(8,128)}, ...), condition=%wide.region_23.24_spmd, body=%wide.region_19.23_spmd.sunk | while | flops 613614336 | bytes 32858372 | solution.py:261
  1359.2 12.7 gather_fusion.3
  1384.7 13.6 gather_fusion.1
  1398.3 448.1 %all-gather.13.cloned.1.call-done = f32[9216,768]{1,0:T(8,128)} async-done(((f32[2304,768]{1,0:T(8,128)}), f32[9216,768]{1,0:T(8,128)}) %all-gather.13.cloned.1.call-update) | async-done | bytes 28311568 | tf_op jit(solution)/shard_map/all_gather | solution.py:16
  1846.5 14.5 reduce_sum.219
  1869.2 9.7 fusion.129
  1881.7 51.2 %while.62 = (s32[]{:T(128)}, bf16[3,768,192]{1,2,0:T(8,128)(2,1)S(1)}, bf16[3,768,192]{1,2,0:T(8,128)(2,1)}, bf16[3,768,192]{1,2,0:T(8,128)(2,1)S(1)}, bf16[3,76...) while((s32[]{:T(128)}, ...), condition=%wide.region_29.30_spmd, body=%wide.region_27.29_spmd.sunk | while | flops 1161510144 | bytes 62592684 | solution.py:281
  1975.7 26.1 all-reduce.3
  2002.3 423.0 %all-gather.11.cloned.1.call-done = f32[9216,768]{1,0:T(8,128)} async-done(((f32[2304,768]{1,0:T(8,128)}), f32[9216,768]{1,0:T(8,128)}) %all-gather.11.cloned.1.call-update) | async-done | bytes 28311568 | tf_op jit(solution)/shard_map/all_gather | solution.py:16
  2425.4 13.8 reduce_sum.218
  2446.0 14.4 reduce-scatter.15.cloned.1.call-done
  2461.9 37.4 %reduce-scatter.13.cloned.1.call-done = bf16[96,576]{1,0:T(8,128)(2,1)} async-done(((bf16[768,576]{1,0:T(8,128)(2,1)}), bf16[96,576]{1,0:T(8,128)(2,1)}) %reduce-scatter.13.cloned.1.call-update) | async-done | bytes 110608
  2501.4 475.7 %all-gather.15.cloned.1.call-done = f32[9216,768]{1,0:T(8,128)} async-done(((f32[2304,768]{1,0:T(8,128)}), f32[9216,768]{1,0:T(8,128)}) %all-gather.15.cloned.1.call-update) | async-done | bytes 28311568 | tf_op jit(solution)/shard_map/all_gather | solution.py:16
  2977.1 13.7 reduce_sum.222
  2998.5 39.9 %all-reduce.2 = (f32[768]{0:T(1024)}, f32[768]{0:T(1024)}, f32[768]{0:T(1024)}, f32[3,768]{1,0:T(4,128)}, f32[3,768]{1,0:T(4,128)}, /*index=5*/f32[3,768]{1,0:T(4,128)}) all-reduce(f32[768]{0:T(1024)S(1)} %get-tuple-element.415, f32[768]{0:T(1024)S(1)} %get-tuple-element.414, ...), channel_id=1, replica_groups=mesh['dp'=8,'tensor'=4] {'dp','tensor'}, use_global_device_ids=true, to_apply=%region_34.35 | all-reduce | flops 9216 | bytes 73728 | tf_op jit(solution)/shard_map/psum | solution.py:342
  3038.4 15.1 add_convert_fusion
  (664 shorter events, 890.3 us)
Async XLA Ops:
  7.2 50.9 %copy-start = (bf16[192,768]{1,0:T(8,128)(2,1)S(1)}, bf16[192,768]{1,0:T(8,128)(2,1)}, u32[]{:S(2)}) copy-start(bf16[192,768]{1,0:T(8,128)(2,1)} %param.40) | copy-start | bytes 884740
  7.2 533.9 %all-gather.9.cloned.1.call-start = ((), (), s32[]{:S(2)}) async-start(), calls=%async_computation.6 | async-start | bytes 35389440 | tf_op jit(solution)/shard_map/all_gather | solution.py:16
  62.1 1784.4 %all-gather.13.cloned.1.call-start = ((), (), s32[]{:S(2)}) async-start(), calls=%async_computation.8 | async-start | bytes 35389440 | tf_op jit(solution)/shard_map/all_gather | solution.py:16
  77.3 13.7 copy-start.45
  91.1 473.0 %copy-start.34 = (f32[768]{0:T(1024)}, f32[768]{0:T(1024)S(1)}, u32[]{:S(2)}) copy-start(f32[768]{0:T(1024)S(1)} %get-tuple-element.540) | copy-start | bytes 9220
  91.1 473.0 %copy-start.36 = (f32[768]{0:T(1024)}, f32[768]{0:T(1024)S(1)}, u32[]{:S(2)}) copy-start(f32[768]{0:T(1024)S(1)} %get-tuple-element.541) | copy-start | bytes 9220
  91.1 473.0 %copy-start.38 = (f32[768]{0:T(1024)}, f32[768]{0:T(1024)S(1)}, u32[]{:S(2)}) copy-start(f32[768]{0:T(1024)S(1)} %get-tuple-element.542) | copy-start | bytes 9220
  91.8 472.3 %copy-start.14 = (f32[2304]{0:T(1024)}, f32[2304]{0:T(1024)S(1)}, u32[]{:S(2)}) copy-start(f32[2304]{0:T(1024)S(1)} %get-tuple-element.416) | copy-start | bytes 27652
  91.9 472.3 %copy-start.16 = (f32[2304]{0:T(1024)}, f32[2304]{0:T(1024)S(1)}, u32[]{:S(2)}) copy-start(f32[2304]{0:T(1024)S(1)} %get-tuple-element.417) | copy-start | bytes 27652
  91.9 472.3 %copy-start.18 = (f32[2304]{0:T(1024)}, f32[2304]{0:T(1024)S(1)}, u32[]{:S(2)}) copy-start(f32[2304]{0:T(1024)S(1)} %get-tuple-element.418) | copy-start | bytes 27652
  564.1 15.6 copy-start.30
  1372.0 599.1 %reduce-scatter.9.cloned.1.call-start = ((), (), s32[]{:S(2)}) async-start(), calls=%async_computation.4 | async-start | bytes 3981312 | tf_op jit(solution)/shard_map/reduce_scatter | solution.py:335
  1377.3 595.8 %reduce-scatter.11.cloned.1.call-start = ((), (), s32[]{:S(2)}) async-start(), calls=%async_computation.5 | async-start | bytes 3981312 | tf_op jit(solution)/shard_map/reduce_scatter | solution.py:338
  1384.6 1040.7 %all-gather.11.cloned.1.call-start = ((), (), s32[]{:S(2)}) async-start(), calls=%async_computation.7 | async-start | bytes 35389440 | tf_op jit(solution)/shard_map/all_gather | solution.py:16
  1398.3 1062.0 %reduce-scatter.15.cloned.1.call-start = ((), (), s32[]{:S(2)}) async-start(), calls=%async_computation.11 | async-start | bytes 442368
  1846.5 14.5 copy-start.15
  1846.5 14.5 copy-start.17
  1846.5 14.5 copy-start.19
  1846.5 14.5 copy-start.35
  1846.5 14.5 copy-start.37
  1846.5 14.5 copy-start.39
  1947.0 552.2 %reduce-scatter.13.cloned.1.call-start = ((), (), s32[]{:S(2)}) async-start(), calls=%async_computation.10 | async-start | bytes 1105920
  1960.0 1017.1 %all-gather.15.cloned.1.call-start = ((), (), s32[]{:S(2)}) async-start(), calls=%async_computation.9 | async-start | bytes 35389440 | tf_op jit(solution)/shard_map/all_gather | solution.py:16
  2990.8 47.6 %copy-start.33 = (f32[768]{0:T(1024)S(1)}, f32[768]{0:T(1024)}, u32[]{:S(2)}) copy-start(f32[768]{0:T(1024)} %param.41) | copy-start | bytes 9220
  (36 other events, 231.5 us)
Sparse Core Ops, SparseCore 0:
  62.2 478.8 all-gather.8
  1372.1 474.3 all-gather.12
  1850.0 46.2 reduce-scatter.8
  1899.7 48.0 reduce-scatter.10
  1949.2 476.1 all-gather.10
  2428.3 32.0 reduce-scatter.14
  2463.5 35.7 reduce-scatter.12
  2501.0 476.1 all-gather.14
